TPU v7x, 256 devices: a whole 4x4x8 slice. The times are simulated.
256 devices in a mesh: section: 16 (over z_hi, x, core), blk: 16 (over y, z_lo).
Axes of the slice: x: 4, y: 4, z: 8 (z_hi: 2, z_lo: 4; z = z_hi * 4 + z_lo), core: 2. Of those that a mesh axis runs over, the one named last changes fastest.
Arguments:
- queries: bfloat16 [16, 2048, 4096], P('section', 'blk'), may hold values from -6 to 6
- key_heads: bfloat16 [16, 2048, 512], P('section', 'blk'), may hold values from -6 to 6
- value_per_head: bfloat16 [16, 2048, 512], P('section', 'blk'), may hold values from -6 to 6
- out_grads: bfloat16 [16, 2048, 4096], P('section', 'blk'), may hold values from -6 to 6
- segment_ids: int32 [16, 2048], P('section', 'blk'), may hold values from 0 to 127, never falling along the last dimension, each value on 1 to 64 neighbouring positions
- block_lists: int32 [16, 16, 4], P('section', 'blk'), may hold values from 0 to 15, as said below
- list_counts: int32 [16, 16], P('section', 'blk'), may hold values from 1 to 4, as said below
Outputs:
- grad_queries: bfloat16 [16, 2048, 4096], P('section', 'blk')
- grad_keys: bfloat16 [16, 2048, 512], P('section', 'blk')
- grad_values: bfloat16 [16, 2048, 512], P('section', 'blk')
Inputs may be any that keep to these rules, and one draw needn't show every extreme that they name: `block_lists`: entry 0 of row b is b itself; for b >= 1 entry 1 is block 0; entries 2 to list_counts - 1 are distinct blocks between 1 and b - 1; entries from list_counts on repeat b. `list_counts`: at least 2 for every query block after the first; the last query block of every micro-batch uses all 4 slots.
All inputs are finite; a program needn't handle non-finite values.
Results may differ from a plain program's by a relative error of at most 0.0051.
Values may be sent and summed in bfloat16 or wider, within the bound.
A program may use at most 64 MiB of HBM per device.

v0:
```python
import math
import jax
import jax.numpy as jnp
from jax import lax
from jax.sharding import PartitionSpec as P

QUERY_HEADS = 32
KEY_VALUE_HEADS = 4
HEAD_SIZE = 128
MASK_BLOCK_SIZE = 128
LIST = 4
NEG_FILL = -1e30


def from_behind(value, axis, by):
    devices = lax.axis_size(axis)
    return lax.ppermute(value, axis, [(i, (i + by) % devices) for i in range(devices)])


def allowed_mask(block_ids, listed_count, query_block, query_segs):
    slot_ok = jnp.arange(LIST, dtype=jnp.int32) < listed_count
    own_block = block_ids == query_block
    positions = jnp.arange(MASK_BLOCK_SIZE, dtype=jnp.int32)
    causal = (positions[None, :] <= positions[:, None]) & (
        query_segs[None, :] == query_segs[:, None]
    )
    earlier = block_ids < query_block
    return slot_ok[None, :, None] & jnp.where(
        own_block[None, :, None], causal[:, None, :], earlier[None, :, None]
    )


def group_terms(query_row_slice, gradient_row_slice, key_rows, value_rows, allowed):
    scale_factor = 1.0 / math.sqrt(HEAD_SIZE)
    scores = (
        jnp.einsum("ihd,ljd->hilj", query_row_slice, key_rows, preferred_element_type=jnp.float32)
        * scale_factor
    )
    scores = jnp.where(allowed[None], scores, NEG_FILL)
    largest = jnp.max(scores, axis=(2, 3), keepdims=True)
    weights = jnp.where(allowed[None], jnp.exp(scores - largest), 0.0)
    probs_full = weights / jnp.sum(weights, axis=(2, 3), keepdims=True)
    dprobs = jnp.einsum(
        "ihd,ljd->hilj", gradient_row_slice, value_rows, preferred_element_type=jnp.float32
    )
    row_delta = jnp.sum(probs_full * dprobs, axis=(2, 3), keepdims=True)
    dscores = (probs_full * (dprobs - row_delta)).astype(jnp.bfloat16)
    probs_half = probs_full.astype(jnp.bfloat16)
    query_grad = (
        jnp.einsum("hilj,ljd->ihd", dscores, key_rows, preferred_element_type=jnp.float32)
        * scale_factor
    )
    key_grad = (
        jnp.einsum("hilj,ihd->ljd", dscores, query_row_slice, preferred_element_type=jnp.float32)
        * scale_factor
    )
    value_grad = jnp.einsum(
        "hilj,ihd->ljd", probs_half, gradient_row_slice, preferred_element_type=jnp.float32
    )
    return (query_grad, key_grad, value_grad)


def per_device(
    queries, key_heads, value_per_head, out_grads, segment_ids, block_lists, list_counts
):
    local_blocks = block_lists.shape[1]
    blk_count = lax.axis_size("blk")
    blocks_all = blk_count * local_blocks
    first_local = lax.axis_index("blk") * local_blocks
    heads_per_group = QUERY_HEADS // KEY_VALUE_HEADS
    key_value_width = KEY_VALUE_HEADS * HEAD_SIZE
    ids_all = block_lists[0]
    flat_ids = ids_all.reshape(-1)
    whole_keys, whole_values = (
        lax.all_gather(key_heads, "blk", axis=1, tiled=True),
        lax.all_gather(value_per_head, "blk", axis=1, tiled=True),
    )
    listed_k = whole_keys[0].reshape(blocks_all, MASK_BLOCK_SIZE, key_value_width)[flat_ids]
    listed_v = whole_values[0].reshape(blocks_all, MASK_BLOCK_SIZE, key_value_width)[flat_ids]
    query_all = queries[0]
    grads_all = out_grads[0]
    segs_all = segment_ids[0]
    counts_all = list_counts[0]
    query_block = first_local + 0
    row_hi = MASK_BLOCK_SIZE
    allowed = allowed_mask(ids_all[0], counts_all[0], query_block, segs_all)
    query_parts = []
    key_parts = []
    value_parts = []
    for shared_key_head in range(KEY_VALUE_HEADS):
        col_lo = shared_key_head * heads_per_group * HEAD_SIZE
        col_hi = col_lo + heads_per_group * HEAD_SIZE
        query_row_slice = query_all[0:row_hi, col_lo:col_hi].reshape(
            MASK_BLOCK_SIZE, heads_per_group, HEAD_SIZE
        )
        gradient_row_slice = grads_all[0:row_hi, col_lo:col_hi].reshape(
            MASK_BLOCK_SIZE, heads_per_group, HEAD_SIZE
        )
        head_keys = listed_k[:, :, shared_key_head * HEAD_SIZE : (shared_key_head + 1) * HEAD_SIZE]
        head_values = listed_v[
            :, :, shared_key_head * HEAD_SIZE : (shared_key_head + 1) * HEAD_SIZE
        ]
        query_grad, key_grad, value_grad = group_terms(
            query_row_slice, gradient_row_slice, head_keys, head_values, allowed
        )
        query_parts.append(query_grad.reshape(MASK_BLOCK_SIZE, heads_per_group * HEAD_SIZE))
        key_parts.append(key_grad)
        value_parts.append(value_grad)
    query_parts_all = jnp.concatenate(query_parts, axis=1).astype(jnp.bfloat16)
    grad_tiles = jnp.concatenate(key_parts + value_parts, axis=2)
    query_gradient_rows = query_parts_all[None]
    placement = (jnp.arange(blocks_all, dtype=jnp.int32)[:, None] == flat_ids[None, :]).astype(
        jnp.float32
    )
    term_all = jnp.einsum("cn,nrw->crw", placement, grad_tiles, precision=lax.Precision.HIGHEST)
    summed = lax.psum_scatter(
        term_all.reshape(blocks_all * MASK_BLOCK_SIZE, 2 * key_value_width),
        "blk",
        scatter_dimension=0,
        tiled=True,
    )
    summed_half = summed.astype(jnp.bfloat16)
    key_grads = summed_half[:, :key_value_width][None]
    value_grads = summed_half[:, key_value_width:][None]
    grad_queries, grad_keys, grad_values = from_behind(
        (query_gradient_rows, key_grads, value_grads), "section", -1
    )
    return (grad_queries, grad_keys, grad_values)


def solution(mesh):
    in_specs = (
        P("section", "blk", None),
        P("section", "blk", None),
        P("section", "blk", None),
        P("section", "blk", None),
        P("section", "blk"),
        P("section", "blk", None),
        P("section", "blk"),
    )
    out_specs = (P("section", "blk", None), P("section", "blk", None), P("section", "blk", None))
    return jax.shard_map(
        per_device, mesh=mesh, in_specs=in_specs, out_specs=out_specs, check_vma=False
    )
```

profile of v0, /device:TPU:1, one launch (start us, length us, event | category | flops | bytes accessed | tf_op | source)
XLA Modules:
  0.0 443.1 jit_solution(12771451435008800897)
XLA Ops:
  7.2 0.7 all-gather.3.cloned.1.call-update
  8.0 0.7 all-gather.5.cloned.1.call-update
  9.4 1.6 copy.22
  11.0 0.7 copy.24
  12.2 79.5 %all-gather.3.cloned.1.call-done = bf16[1,2048,512]{2,1,0:T(8,128)(2,1)} async-done(((bf16[1,128,512]{2,1,0:T(8,128)(2,1)}), bf16[1,2048,512]{2,1,0:T(8,128)(2,1)}) %all-gather.3.cloned.1.call-update) | async-done | bytes 2097168 | tf_op jit(solution)/shard_map/all_gather | solution.py:75
  91.7 2.2 gather_fusion
  93.8 86.1 %all-gather.5.cloned.1.call-done = bf16[1,2048,512]{2,1,0:T(8,128)(2,1)} async-done(((bf16[1,128,512]{2,1,0:T(8,128)(2,1)}), bf16[1,2048,512]{2,1,0:T(8,128)(2,1)}) %all-gather.5.cloned.1.call-update) | async-done | bytes 2097168 | tf_op jit(solution)/shard_map/all_gather | solution.py:76
  179.9 2.2 gather_fusion.1
  182.1 0.4 fusion.50
  182.5 0.4 fusion.51
  182.9 0.4 fusion.49
  183.4 0.4 fusion.44
  183.8 0.4 fusion.12
  184.3 0.5 fusion.17
  184.8 0.7 fusion.38
  185.5 1.7 fusion.9
  187.2 0.5 fusion.19
  187.7 0.7 fusion.36
  188.4 1.8 fusion.6
  190.2 0.7 fusion.32
  190.9 0.7 fusion.34
  191.6 1.4 fusion.3
  193.0 2.4 fusion.11
  195.5 0.4 fusion.64
  195.9 0.4 fusion.67
  196.4 0.4 fusion.65
  196.8 0.7 fusion.5
  197.6 0.4 fusion.66
  198.2 0.3 fusion.42
  198.5 0.3 fusion.41
  198.8 0.3 fusion.40
  200.0 4.0 fusion.54
  204.1 8.3 %copy.44 = f32[16,128,1024]{2,1,0:T(8,128)} copy(f32[16,128,1024]{2,0,1:T(8,128)S(1)} %fusion.54) | data formatting | bytes 16777216 | tf_op jit(solution)/shard_map/cn,nrw->crw/dot_general | solution.py:115
  212.4 1.2 fusion.31
  213.6 0.9 copy.40
  214.5 1.2 fusion.28
  215.8 0.9 copy.43
  216.6 1.3 fusion.29
  218.1 1.2 fusion.30
  219.6 10.1 %collective-permute-start = (bf16[1,128,4096]{2,1,0:T(8,128)(2,1)S(1)}, bf16[1,128,4096]{2,1,0:T(8,128)(2,1)S(1)}, u32[]{:S(2)}, u32[]{:S(2)}) collective-permute-start(bf16[1,128,4096]{2,1,0:T(8,128)(2,1)S(1)} %pad_maximum_fusion), channel_id=1, source_target_pairs={{0,240},{16,0},{32,16},{48,32},{64,48},{80,64},{96,80},{112,96},{1... | collective-permute-start | bytes 3145736 | tf_op jit(solution)/shard_map/ppermute | solution.py:17
  229.6 197.7 %reduce-scatter.2.cloned.1.call-done = f32[128,1024]{1,0:T(8,128)} async-done(((f32[2048,1024]{1,0:T(8,128)}), f32[128,1024]{1,0:T(8,128)}) %reduce-scatter.2.cloned.1.call-update) | async-done | bytes 524304 | tf_op jit(solution)/shard_map/reduce_scatter | solution.py:116
  427.3 1.1 convert_element_type.44
  428.4 0.5 collective-permute-start.2
  429.0 3.9 collective-permute-done.2
  432.9 1.4 collective-permute-done.1
  434.3 1.0 copy.116
  435.3 0.7 copy.117
  435.9 0.7 copy.118
  (51 shorter events, 2.2 us)
Async XLA Ops:
  7.2 3.8 copy-start.9
  7.2 84.5 %all-gather.3.cloned.1.call-start = ((), (), s32[]{:S(2)}) async-start(), calls=%async_computation.1 | async-start | bytes 2228224 | tf_op jit(solution)/shard_map/all_gather | solution.py:75
  7.9 172.0 %all-gather.5.cloned.1.call-start = ((), (), s32[]{:S(2)}) async-start(), calls=%async_computation.2 | async-start | bytes 2228224 | tf_op jit(solution)/shard_map/all_gather | solution.py:76
  8.7 418.6 %reduce-scatter.2.cloned.1.call-start = ((), (), s32[]{:S(2)}) async-start(), calls=%async_computation.3 | async-start | bytes 8912896 | tf_op jit(solution)/shard_map/reduce_scatter | solution.py:116
  9.4 2.3 copy-start.13
  9.4 2.4 copy-start.12
  12.0 170.5 %copy-start.5 = (bf16[128,1024]{0,1:T(8,128)(2,1)}, bf16[128,1024]{0,1:T(8,128)(2,1)S(1)}, u32[]{:S(2)}) copy-start(bf16[128,1024]{0,1:T(8,128)(2,1)S(1)} %get-tuple-element.12) | copy-start | bytes 786436
  12.1 170.9 %copy-start.3 = (bf16[128,1024]{0,1:T(8,128)(2,1)}, bf16[128,1024]{0,1:T(8,128)(2,1)S(1)}, u32[]{:S(2)}) copy-start(bf16[128,1024]{0,1:T(8,128)(2,1)S(1)} %get-tuple-element.14) | copy-start | bytes 786436
  12.1 171.7 %copy-start.7 = (bf16[128,1024]{0,1:T(8,128)(2,1)}, bf16[128,1024]{0,1:T(8,128)(2,1)S(1)}, u32[]{:S(2)}) copy-start(bf16[128,1024]{0,1:T(8,128)(2,1)S(1)} %get-tuple-element.15) | copy-start | bytes 786436
  93.8 90.0 %copy-start.2 = (bf16[4,128,512]{2,1,0:T(8,128)(2,1)}, bf16[4,128,512]{2,1,0:T(8,128)(2,1)S(1)}, u32[]{:S(2)}) copy-start(bf16[4,128,512]{2,1,0:T(8,128)(2,1)S(1)} %gather_fusion) | copy-start | bytes 1572868
  193.0 2.5 copy-start.8
  193.0 2.9 copy-start.6
  195.4 1.0 copy-start.4
  197.6 1.7 copy-start
  213.6 3.0 copy-start.1
  216.6 2.9 copy-start.10
  217.9 1.6 copy-start.11
  219.6 209.4 %collective-permute-start = (bf16[1,128,4096]{2,1,0:T(8,128)(2,1)S(1)}, bf16[1,128,4096]{2,1,0:T(8,128)(2,1)S(1)}, u32[]{:S(2)}, u32[]{:S(2)}) collective-permute-start(bf16[1,128,4096]{2,1,0:T(8,128)(2,1)S(1)} %pad_maximum_fusion), channel_id=1, source_target_pairs={{0,240},{16,0},{32,16},{48,32},{64,48},{80,64},{96,80},{112,96},{1... | collective-permute-start | bytes 3145736 | tf_op jit(solution)/shard_map/ppermute | solution.py:17
  428.4 4.5 %collective-permute-start.2 = (bf16[1,128,512]{2,1,0:T(8,128)(2,1)S(1)}, bf16[1,128,512]{2,1,0:T(8,128)(2,1)S(1)}, u32[]{:S(2)}, u32[]{:S(2)}) collective-permute-start(bf16[1,128,512]{2,1,0:T(8,128)(2,1)S(1)} %get-tuple-element.20), channel_id=1, source_target_pairs={{0,240},{16,0},{32,16},{48,32},{64,48},{80,64},{96,80},{112,96},{1... | collective-permute-start | bytes 393224 | tf_op jit(solution)/shard_map/ppermute | solution.py:17
  428.9 5.4 %collective-permute-start.1 = (bf16[1,128,512]{2,1,0:T(8,128)(2,1)S(1)}, bf16[1,128,512]{2,1,0:T(8,128)(2,1)S(1)}, u32[]{:S(2)}, u32[]{:S(2)}) collective-permute-start(bf16[1,128,512]{2,1,0:T(8,128)(2,1)S(1)} %get-tuple-element.21), channel_id=1, source_target_pairs={{0,240},{16,0},{32,16},{48,32},{64,48},{80,64},{96,80},{112,96},{1... | collective-permute-start | bytes 393224 | tf_op jit(solution)/shard_map/ppermute | solution.py:17
Sparse Core Ops, SparseCore 0:
  9.8 81.8 all-gather.2
  93.4 86.4 all-gather.4
  212.5 214.7 reduce-scatter.1
where the time goes:
time: 443 us
  waiting for transfers between devices  370 us (84%)
  matrix products  20.5 us (5%)
  local copies, waits for them, and re-layouts  20.4 us (5%)
  between operations  14.9 us (3%)
  starting transfers between devices  10.8 us (2%)
  other arithmetic  6.55 us (1%)
    reduce_scatter x1, waiting for transfers between devices, per_device(): lax.psum_scatter(term_all.reshape(blocks_all * MASK_BLOCK_SIZE, 2 * key_v...  198 us
    all_gather x1, waiting for transfers between devices, per_device(): lax.all_gather(value_per_head, 'blk', axis=1, tiled=True)  86.1 us
    all_gather x1, waiting for transfers between devices, per_device(): lax.all_gather(key_heads, 'blk', axis=1, tiled=True)  79.5 us
    ppermute x3, starting transfers between devices, from_behind(): lax.ppermute(value, axis, [(i, (i + by) % devices) for i in range(devices)])  10.6 us
  transfers between devices with their start and end apart: 6, of which 5 were waited for; matrix products, arithmetic and copies ran while one was open for 3% of the time, Pallas kernels for 0%

commit v1 on v0

--- a/solution.py
+++ b/solution.py
@@ -73,7 +73,9 @@
     flat_ids = ids_all.reshape(-1)
     whole_keys, whole_values = (
         lax.all_gather(key_heads, "blk", axis=1, tiled=True),
-        lax.all_gather(value_per_head, "blk", axis=1, tiled=True),
+        jnp.concatenate(
+            lax.all_to_all(jnp.stack([value_per_head] * lax.axis_size("blk")), "blk", 0, 0), axis=1
+        ),
     )
     listed_k = whole_keys[0].reshape(blocks_all, MASK_BLOCK_SIZE, key_value_width)[flat_ids]
     listed_v = whole_values[0].reshape(blocks_all, MASK_BLOCK_SIZE, key_value_width)[flat_ids]

time: 443 us -> 384 us (0.87)
  waiting for transfers between devices: 370 us -> 291 us
  local copies, waits for them, and re-layouts: 20.4 us -> 27.5 us
  starting transfers between devices: 10.8 us -> 16.8 us
    all_gather x1 -> x0, waiting for transfers between devices: 86.1 us -> none  [per_device(): lax.all_gather(value_per_head, 'blk', axis=1, tiled=True)]
    all_to_all x0 -> x1, starting transfers between devices: none -> 9.37 us  [per_device(): lax.all_to_all(jnp.stack([value_per_head] * lax.axis_size('blk')), 'blk',...]
    all_gather x1, waiting for transfers between devices: 79.5 us -> 88.5 us  [per_device(): lax.all_gather(key_heads, 'blk', axis=1, tiled=True)]
  transfers between devices with their start and end apart: 6 -> 6, of which waited for: 5 -> 4; matrix products, arithmetic and copies ran while one was open for 3% -> 5% of each run, Pallas kernels for 0% -> 0%
where the time goes in v1:
time: 384 us; the launch traced here: 382 us
  waiting for transfers between devices  291 us (76%)
  local copies, waits for them, and re-layouts  27.5 us (7%)
  matrix products  24.1 us (6%)
  starting transfers between devices  16.8 us (4%)
  between operations  15.4 us (4%)
  other arithmetic  6.54 us (2%)
    reduce_scatter x1, waiting for transfers between devices, per_device(): lax.psum_scatter(term_all.reshape(blocks_all * MASK_BLOCK_SIZE, 2 * key_v...  197 us
    all_gather x1, waiting for transfers between devices, per_device(): lax.all_gather(key_heads, 'blk', axis=1, tiled=True)  88.5 us
    all_to_all x1, starting transfers between devices, per_device(): lax.all_to_all(jnp.stack([value_per_head] * lax.axis_size('blk')), 'blk',...  9.37 us
    dot_general x1, local copies, waits for them, and re-layouts, per_device(): jnp.einsum('cn,nrw->crw', placement, grad_tiles, precision=lax.Precision....  8.3 us
    unnamed x58, local copies, waits for them, and re-layouts  8.1 us
  transfers between devices with their start and end apart: 6, of which 4 were waited for; matrix products, arithmetic and copies ran while one was open for 5% of the time, Pallas kernels for 0%

profile of v1, /device:TPU:1, one launch (start us, length us, event | category | flops | bytes accessed | tf_op | source)
XLA Modules:
  0.0 381.6 jit_solution(6409033894757070523)
XLA Ops:
  7.2 0.7 all-gather.2.cloned.1.call-update
  7.9 2.4 stack.2
  10.3 9.4 %all-to-all-start = ((bf16[16,1,128,512]{3,2,1,0:T(8,128)(2,1)}), bf16[16,1,128,512]{3,2,1,0:T(8,128)(2,1)}, u32[]{:S(2)}, u32[]{:S(2)}) async-start(bf16[16,1,128,512]{3,2,1,0:T(8,128)(2,1)} %stack.2), calls=%async_computation | async-start | bytes 4194304 | tf_op jit(solution)/shard_map/all_to_all | solution.py:77
  20.5 0.7 copy.22
  21.2 0.7 copy.24
  22.2 0.9 fusion.62
  23.0 1.1 fusion.63
  24.1 88.5 %all-gather.2.cloned.1.call-done = bf16[1,2048,512]{2,1,0:T(8,128)(2,1)} async-done(((bf16[1,128,512]{2,1,0:T(8,128)(2,1)}), bf16[1,2048,512]{2,1,0:T(8,128)(2,1)}) %all-gather.2.cloned.1.call-update) | async-done | bytes 2097168 | tf_op jit(solution)/shard_map/all_gather | solution.py:75
  112.6 2.2 gather_fusion
  114.8 1.7 fusion.50
  116.6 1.8 fusion.51
  118.8 3.0 gather_fusion.1
  121.8 1.3 fusion.44
  123.1 0.4 fusion.12
  123.6 0.5 fusion.17
  124.2 0.7 fusion.38
  124.9 0.9 copy-done.6
  125.7 0.6 copy-done.7
  126.4 1.7 fusion.9
  128.1 0.5 fusion.19
  129.1 0.7 fusion.36
  129.8 1.8 fusion.6
  131.6 0.7 fusion.32
  132.5 0.7 fusion.34
  133.2 1.4 fusion.3
  134.6 2.4 fusion.11
  137.1 0.4 fusion.64
  137.6 0.4 fusion.67
  138.2 0.4 fusion.65
  138.7 0.7 fusion.5
  139.4 0.4 fusion.66
  141.9 4.0 %fusion.54 = f32[16,128,1024]{2,0,1:T(8,128)S(1)} fusion(f32[4,128,1024]{2,0,1:T(4,128)S(1)} %bitcast_dynamic-update-slice_fusion, s32[4]{0:T(128)S(1)} %bitcast.346), kind=kOutput, calls=%fused_computation.100 | convolution fusion | flops 100663360 | bytes 10485776 | tf_op jit(solution)/shard_map/cn,nrw->crw/dot_general | solution.py:117
  145.9 8.3 %copy.44 = f32[16,128,1024]{2,1,0:T(8,128)} copy(f32[16,128,1024]{2,0,1:T(8,128)S(1)} %fusion.54) | data formatting | bytes 16777216 | tf_op jit(solution)/shard_map/cn,nrw->crw/dot_general | solution.py:117
  154.3 1.2 copy-done.3
  155.5 1.3 fusion.31
  156.8 0.9 copy.40
  157.7 1.2 fusion.28
  159.1 1.3 fusion.29
  160.5 1.2 fusion.30
  162.0 6.8 %collective-permute-start = (bf16[1,128,4096]{2,1,0:T(8,128)(2,1)S(1)}, bf16[1,128,4096]{2,1,0:T(8,128)(2,1)S(1)}, u32[]{:S(2)}, u32[]{:S(2)}) collective-permute-start(bf16[1,128,4096]{2,1,0:T(8,128)(2,1)S(1)} %pad_maximum_fusion), channel_id=1, source_target_pairs={{0,240},{16,0},{32,16},{48,32},{64,48},{80,64},{96,80},{112,96},{1... | collective-permute-start | bytes 3145736 | tf_op jit(solution)/shard_map/ppermute | solution.py:17
  168.8 196.7 %reduce-scatter.2.cloned.1.call-done = f32[128,1024]{1,0:T(8,128)} async-done(((f32[2048,1024]{1,0:T(8,128)}), f32[128,1024]{1,0:T(8,128)}) %reduce-scatter.2.cloned.1.call-update) | async-done | bytes 524304 | tf_op jit(solution)/shard_map/reduce_scatter | solution.py:118
  365.5 1.1 convert_element_type.44
  366.6 0.4 collective-permute-start.2
  367.2 3.9 %collective-permute-done.2 = bf16[1,128,512]{2,1,0:T(8,128)(2,1)S(1)} collective-permute-done((bf16[1,128,512]{2,1,0:T(8,128)(2,1)S(1)}, bf16[1,128,512]{2,1,0:T(8,128)(2,1)S(1)}, u32[]{:S(2)}, u32[]{:S(2)}) %collective-permute-start.2) | collective-permute-done | bytes 131104 | tf_op jit(solution)/shard_map/ppermute | solution.py:17
  371.1 1.4 collective-permute-done.1
  372.5 1.0 copy.116
  373.5 0.7 copy.117
  374.1 0.7 copy.118
  (73 shorter events, 4.4 us)
Async XLA Ops:
  7.2 105.5 %all-gather.2.cloned.1.call-start = ((), (), s32[]{:S(2)}) async-start(), calls=%async_computation.2 | async-start | bytes 2228224 | tf_op jit(solution)/shard_map/all_gather | solution.py:75
  10.3 10.2 %copy-start.15 = (bf16[1,128,4096]{2,1,0:T(8,128)(2,1)S(1)}, bf16[1,128,4096]{2,1,0:T(8,128)(2,1)}, u32[]{:S(2)}) copy-start(bf16[1,128,4096]{2,1,0:T(8,128)(2,1)} %param.7) | copy-start | bytes 3145732
  10.3 108.4 %all-to-all-start = ((bf16[16,1,128,512]{3,2,1,0:T(8,128)(2,1)}), bf16[16,1,128,512]{3,2,1,0:T(8,128)(2,1)}, u32[]{:S(2)}, u32[]{:S(2)}) async-start(bf16[16,1,128,512]{3,2,1,0:T(8,128)(2,1)} %stack.2), calls=%async_computation | async-start | bytes 4194304 | tf_op jit(solution)/shard_map/all_to_all | solution.py:77
  19.7 1.5 copy-start.16
  19.7 345.8 %reduce-scatter.2.cloned.1.call-start = ((), (), s32[]{:S(2)}) async-start(), calls=%async_computation.3 | async-start | bytes 8912896 | tf_op jit(solution)/shard_map/reduce_scatter | solution.py:118
  20.5 1.4 copy-start.24
  20.5 1.4 copy-start.23
  23.0 93.5 %copy-start.11 = (bf16[128,1024]{0,1:T(8,128)(2,1)}, bf16[128,1024]{0,1:T(8,128)(2,1)S(1)}, u32[]{:S(2)}) copy-start(bf16[128,1024]{0,1:T(8,128)(2,1)S(1)} %get-tuple-element.12) | copy-start | bytes 786436
  114.8 8.3 %copy-start.8 = (bf16[4,128,512]{2,1,0:T(8,128)(2,1)}, bf16[4,128,512]{2,1,0:T(8,128)(2,1)S(1)}, u32[]{:S(2)}) copy-start(bf16[4,128,512]{2,1,0:T(8,128)(2,1)S(1)} %gather_fusion) | copy-start | bytes 1572868
  114.8 3.5 copy-start.9
  118.3 3.5 copy-start.17
  118.8 4.4 %copy-start.13 = (bf16[128,1024]{0,1:T(8,128)(2,1)S(1)}, bf16[128,1024]{0,1:T(8,128)(2,1)}, u32[]{:S(2)}) copy-start(bf16[128,1024]{0,1:T(8,128)(2,1)} %get-tuple-element.15) | copy-start | bytes 786436
  123.1 1.0 copy-start.22
  124.1 1.6 copy-start.6
  124.1 2.2 copy-start.7
  124.1 2.3 copy-start.19
  128.1 1.0 copy-start.21
  131.6 1.0 copy-start.20
  134.6 2.5 copy-start.14
  134.6 2.9 copy-start.12
  137.1 1.6 copy-start
  137.1 1.6 copy-start.2
  137.1 1.2 copy-start.10
  139.4 1.7 copy-start.4
  154.2 1.2 copy-start.3
  155.5 2.2 copy-start.1
  156.8 2.3 copy-start.5
  159.1 2.8 copy-start.18
  162.0 205.1 %collective-permute-start = (bf16[1,128,4096]{2,1,0:T(8,128)(2,1)S(1)}, bf16[1,128,4096]{2,1,0:T(8,128)(2,1)S(1)}, u32[]{:S(2)}, u32[]{:S(2)}) collective-permute-start(bf16[1,128,4096]{2,1,0:T(8,128)(2,1)S(1)} %pad_maximum_fusion), channel_id=1, source_target_pairs={{0,240},{16,0},{32,16},{48,32},{64,48},{80,64},{96,80},{112,96},{1... | collective-permute-start | bytes 3145736 | tf_op jit(solution)/shard_map/ppermute | solution.py:17
  366.6 4.5 %collective-permute-start.2 = (bf16[1,128,512]{2,1,0:T(8,128)(2,1)S(1)}, bf16[1,128,512]{2,1,0:T(8,128)(2,1)S(1)}, u32[]{:S(2)}, u32[]{:S(2)}) collective-permute-start(bf16[1,128,512]{2,1,0:T(8,128)(2,1)S(1)} %get-tuple-element.20), channel_id=1, source_target_pairs={{0,240},{16,0},{32,16},{48,32},{64,48},{80,64},{96,80},{112,96},{1... | collective-permute-start | bytes 393224 | tf_op jit(solution)/shard_map/ppermute | solution.py:17
  367.1 5.4 %collective-permute-start.1 = (bf16[1,128,512]{2,1,0:T(8,128)(2,1)S(1)}, bf16[1,128,512]{2,1,0:T(8,128)(2,1)S(1)}, u32[]{:S(2)}, u32[]{:S(2)}) collective-permute-start(bf16[1,128,512]{2,1,0:T(8,128)(2,1)S(1)} %get-tuple-element.21), channel_id=1, source_target_pairs={{0,240},{16,0},{32,16},{48,32},{64,48},{80,64},{96,80},{112,96},{1... | collective-permute-start | bytes 393224 | tf_op jit(solution)/shard_map/ppermute | solution.py:17
Sparse Core Ops, SparseCore 0:
  9.8 102.7 all-gather.1
  154.4 211.0 reduce-scatter.1
